TPU v7x, 32 devices: a whole 2x2x4 slice. The times are simulated.
32 devices in a mesh: segment: 4 (over z), ctx: 4 (over y, x), tp: 2 (over core).
Axes of the slice: x: 2, y: 2, z: 4, core: 2. Of those that a mesh axis runs over, the one named last changes fastest.
Arguments:
- queries: bfloat16 [4, 512, 8, 640], P('segment', 'ctx', 'tp'), may hold values from -200 to 200
- pairs: bfloat16 [4, 512, 8, 256], P('segment', 'ctx', 'tp'), may hold values from -6 to 6
- out_proj: bfloat16 [4, 8, 640, 5120], P('segment', 'tp'), may hold values from -0.625 to 0.625
- lengths: int32 [4, 4], replicated, may hold values from 1 to 256, 512 in all within a row
Outputs:
- scored: bfloat16 [4, 512, 5120], P('segment', 'ctx', 'tp')
Inputs may be any that keep to these rules, and one draw needn't show every extreme that they name: `lengths`: each row sums to 512; its largest length is exactly 256.
All inputs are finite; a program needn't handle non-finite values.
Results may differ from a plain program's by a relative error of at most 0.014.
Values may be sent and summed in bfloat16 or wider, within the bound.
A program may use at most 64 MiB of HBM per device.

v0:
```python
import math
import jax
import jax.numpy as jnp
from jax import lax
from jax.sharding import PartitionSpec as P


def from_behind(value, axis, by):
    size = lax.axis_size(axis)
    return lax.ppermute(value, axis, [(i, (i + by) % size) for i in range(size)])


def rollout_ids(positions, row_lengths):
    row_ends = jnp.cumsum(row_lengths)
    return jnp.sum((positions[:, None] >= row_ends[None, :]).astype(jnp.int32), axis=1)


def attend(query_shard, pair_shard, row_lengths):
    rows_here = query_shard.shape[1]
    local_heads = pair_shard.shape[2]
    head_dim = pair_shard.shape[3] // 2
    group_size = query_shard.shape[3] // head_dim
    first_pos = lax.axis_index("ctx") * rows_here
    query_pos = first_pos + jnp.arange(rows_here, dtype=jnp.int32)
    query_rollout = rollout_ids(query_pos, row_lengths)
    query_heads = query_shard[0].reshape(rows_here, local_heads, group_size, head_dim)
    score_scale = 1.0 / math.sqrt(head_dim)

    def update(state_in, key_block, key_begin):
        running_max, denom, accum = state_in
        block_len = key_block.shape[0]
        key_pos = key_begin + jnp.arange(block_len, dtype=jnp.int32)
        key_rollout = rollout_ids(key_pos, row_lengths)
        visible = (query_rollout[:, None] == key_rollout[None, :]) & (
            key_pos[None, :] <= query_pos[:, None]
        )
        scores = (
            jnp.einsum(
                "rhgd,khd->hgrk",
                query_heads,
                key_block[:, :, :head_dim],
                preferred_element_type=jnp.float32,
            )
            * score_scale
        )
        scores = jnp.where(visible, scores, -1e30)
        new_max = jnp.maximum(running_max, jnp.max(scores, axis=-1))
        rescale = jnp.exp(running_max - new_max)
        weights = jnp.where(visible, jnp.exp(scores - new_max[..., None]), 0.0)
        denom = denom * rescale + jnp.sum(weights, axis=-1)
        added = jnp.einsum(
            "hgrk,khd->hgrd",
            weights.astype(jnp.bfloat16),
            key_block[:, :, head_dim:],
            preferred_element_type=jnp.float32,
        )
        accum = accum * rescale[..., None] + added
        return (new_max, denom, accum)

    starting = (
        jnp.full((local_heads, group_size, rows_here), -1e30, jnp.float32),
        jnp.zeros((local_heads, group_size, rows_here), jnp.float32),
        jnp.zeros((local_heads, group_size, rows_here, head_dim), jnp.float32),
    )
    shards = lax.all_gather(pair_shard[0], "ctx", axis=0, tiled=True)
    shard_rows = shards.shape[0]
    block_len = math.gcd(shard_rows, 512)

    def one_step(step_index, inner):
        key_block = lax.dynamic_slice_in_dim(shards, step_index * block_len, block_len, 0)
        return update(inner, key_block, step_index * block_len)

    running_max, denom, accum = lax.fori_loop(0, shard_rows // block_len, one_step, starting)
    outputs = accum / denom[..., None]
    outputs = jnp.transpose(outputs, (2, 0, 1, 3)).reshape(
        1, rows_here, local_heads, group_size * head_dim
    )
    return outputs.astype(jnp.bfloat16)


def local(queries, pairs, out_proj, lengths):
    section = lax.axis_index("segment")
    own_result = attend(queries, pairs, lengths[section])
    attended = from_behind(own_result, "segment", -1)
    rows_here = attended.shape[1]
    partial_sum = jnp.dot(
        attended.reshape(rows_here, -1),
        out_proj[0].reshape(-1, out_proj.shape[3]),
        preferred_element_type=jnp.float32,
    )
    shares = lax.psum_scatter(
        partial_sum.astype(jnp.bfloat16), "tp", scatter_dimension=1, tiled=True
    )
    return shares.reshape(1, rows_here, -1)


def solution(mesh):
    return jax.shard_map(
        local,
        mesh=mesh,
        in_specs=(
            P("segment", "ctx", "tp", None),
            P("segment", "ctx", "tp", None),
            P("segment", "tp", None, None),
            P(),
        ),
        out_specs=P("segment", "ctx", "tp"),
        check_vma=False,
    )
```

profile of v0, /device:TPU:0, one launch (start us, length us, event | category | flops | bytes accessed | tf_op | source)
XLA Modules:
  0.0 89.1 jit_solution(15405422814970957084)
XLA Ops:
  6.5 0.0 copy-start
  6.5 0.0 all-gather.3.cloned.1.call-start
  6.5 1.7 %copy.16 = bf16[1,128,4,256]{3,1,2,0:T(8,128)(2,1)} copy(bf16[1,128,4,256]{3,2,1,0:T(4,128)(2,1)} %param.5) | data formatting | bytes 524288 | tf_op args[1]
  8.2 0.0 all-gather.3.cloned.1.call-update
  8.3 0.0 reduce-scatter.2.cloned.1.call-start
  8.3 0.0 copy-done
  8.3 0.2 reduce-window.8
  8.5 1.6 %copy.17 = bf16[1,128,4,640]{1,3,2,0:T(8,128)(2,1)S(1)} copy(bf16[1,128,4,640]{3,2,1,0:T(4,128)(2,1)} %param.4) | data formatting | bytes 1310720 | tf_op args[0]
  10.1 0.1 convert_reduce_fusion
  10.2 0.1 convert_reduce_fusion.1
  10.3 0.1 fusion.24
  10.4 28.0 %all-gather.3.cloned.1.call-done = bf16[1,512,4,256]{3,1,2,0:T(8,128)(2,1)} async-done(((bf16[1,128,4,256]{3,1,2,0:T(8,128)(2,1)}), bf16[1,512,4,256]{3,1,2,0:T(8,128)(2,1)}) %all-gather.3.cloned.1.call-update) | async-done | bytes 1048592 | tf_op jit(solution)/shard_map/all_gather | solution.py:65
  38.4 0.0 copy-start.1
  38.4 2.0 %fusion.8 = (f32[4,5,128]{2,1,0:T(8,128)S(1)}, f32[4,512,128,5]{2,1,3,0:T(8,128)S(1)}) fusion(pred[128,512]{0,1:T(8,128)(4,1)S(1)} %fusion.24, bf16[128,4,5,128]{0,3,2,1:T(8,128)(2,1)S(1)} %bitcast.63, bf16[512,4,256]{2,0,1:T(8,128)(2,1)} %bitcast.65), kind=kOutput, calls=%fused_computation.6 | convolution fusion | flops 339473920 | bytes 6498304 | tf_op jit(solution)/shard_map/while/body/eval_jaxpr/rhgd,khd->hgrk/dot_general | solution.py:38
  40.5 1.3 %fusion.9 = f32[4,5,128]{2,1,0:T(8,128)S(1)} fusion(f32[4,512,128,5]{2,1,3,0:T(8,128)S(1)} %get-tuple-element.26, f32[4,5,128]{2,1,0:T(8,128)S(1)} %get-tuple-element.24, pred[128,512]{0,1:T(8,128)(4,1)S(1)} %fusion.24), kind=kLoop, calls=%fused_computation.7 | loop fusion | flops 6551040 | bytes 5328896 | tf_op jit(solution)/shard_map/while/body/eval_jaxpr/reduce_sum | solution.py:50
  41.8 0.0 copy-done.1
  41.8 1.5 %divide_convert_fusion = bf16[128,4,5,128]{0,3,2,1:T(8,128)(2,1)S(1)} fusion(f32[4,512,128,5]{2,1,3,0:T(8,128)S(1)} %get-tuple-element.26, f32[4,5,128]{2,1,0:T(8,128)S(1)} %get-tuple-element.24, pred[128,512]{0,1:T(8,128)(4,1)S(1)} %fusion.24, f32[128,4,5]{0,2,1:T(8,128)S(1)} %bitcast_add_fusion, f32[128,4,5]{0,2,1:T(8,128)S(1)} %get-tuple-element.23, ...), kind=kOutput, calls=%fused_computation.13 | convolution fusion | flops 343080960 | bytes 6537216 | tf_op jit(solution)/shard_map/while/body/eval_jaxpr/hgrk,khd->hgrd/dot_general | solution.py:51
  43.3 0.3 copy.21
  43.6 3.4 %collective-permute-start = (bf16[1,128,4,640]{3,1,2,0:T(8,128)(2,1)S(1)}, bf16[1,128,4,640]{3,1,2,0:T(8,128)(2,1)S(1)}, u32[]{:S(2)}, u32[]{:S(2)}) collective-permute-start(bf16[1,128,4,640]{3,1,2,0:T(8,128)(2,1)S(1)} %copy.21), channel_id=1, source_target_pairs={{0,24},{8,0},{16,8},{24,16},{1,25},{9,1},{17,9},{25,17},{2,26},{10... | collective-permute-start | bytes 1966088 | tf_op jit(solution)/shard_map/ppermute | solution.py:10
  47.0 13.8 %collective-permute-done = bf16[1,128,4,640]{3,1,2,0:T(8,128)(2,1)S(1)} collective-permute-done((bf16[1,128,4,640]{3,1,2,0:T(8,128)(2,1)S(1)}, bf16[1,128,4,640]{3,1,2,0:T(8,128)(2,1)S(1)}, u32[]{:S(2)}, u32[]{:S(2)}) %collective-permute-start) | collective-permute-done | bytes 655392 | tf_op jit(solution)/shard_map/ppermute | solution.py:10
  60.8 11.7 %fusion.5 = bf16[128,5120]{1,0:T(8,128)(2,1)} fusion(bf16[1,4,640,5120]{3,2,1,0:T(8,128)(2,1)} %param.6, bf16[1,128,4,640]{3,1,2,0:T(8,128)(2,1)S(1)} %collective-permute-done), kind=kOutput, calls=%fused_computation.3 | convolution fusion | flops 3356098560 | bytes 28180480 | tf_op jit(solution)/shard_map/dot_general | solution.py:86
  72.5 0.0 reduce-scatter.2.cloned.1.call-update
  72.6 9.7 %reduce-scatter.2.cloned.1.call-done = bf16[128,2560]{1,0:T(8,128)(2,1)} async-done(((bf16[128,5120]{1,0:T(8,128)(2,1)}), bf16[128,2560]{1,0:T(8,128)(2,1)}) %reduce-scatter.2.cloned.1.call-update) | async-done | bytes 655376 | tf_op jit(solution)/shard_map/reduce_scatter | solution.py:91
  (4 shorter events, 0.0 us)
Async XLA Ops:
  6.5 1.8 %copy-start = (s32[4,4]{1,0:T(4,128)S(1)}, s32[4,4]{1,0:T(4,128)}, u32[]{:S(2)}) copy-start(s32[4,4]{1,0:T(4,128)} %param.7) | copy-start | bytes 196
  6.5 31.9 %all-gather.3.cloned.1.call-start = ((), (), s32[]{:S(2)}) async-start(), calls=%async_computation.2 | async-start | bytes 1310720 | tf_op jit(solution)/shard_map/all_gather | solution.py:65
  8.3 74.0 %reduce-scatter.2.cloned.1.call-start = ((), (), s32[]{:S(2)}) async-start(), calls=%async_computation.1 | async-start | bytes 1966080 | tf_op jit(solution)/shard_map/reduce_scatter | solution.py:91
  38.4 3.3 %copy-start.1 = (bf16[1,512,4,256]{3,1,2,0:T(8,128)(2,1)S(1)}, bf16[1,512,4,256]{3,1,2,0:T(8,128)(2,1)}, u32[]{:S(2)}) copy-start(bf16[1,512,4,256]{3,1,2,0:T(8,128)(2,1)} %all-gather.3.cloned.1.call-done) | copy-start | bytes 3145732
  43.6 17.2 %collective-permute-start = (bf16[1,128,4,640]{3,1,2,0:T(8,128)(2,1)S(1)}, bf16[1,128,4,640]{3,1,2,0:T(8,128)(2,1)S(1)}, u32[]{:S(2)}, u32[]{:S(2)}) collective-permute-start(bf16[1,128,4,640]{3,1,2,0:T(8,128)(2,1)S(1)} %copy.21), channel_id=1, source_target_pairs={{0,24},{8,0},{16,8},{24,16},{1,25},{9,1},{17,9},{25,17},{2,26},{10... | collective-permute-start | bytes 1966088 | tf_op jit(solution)/shard_map/ppermute | solution.py:10
Sparse Core Ops, SparseCore 0:
  9.2 29.2 all-gather.2
  72.7 9.5 reduce-scatter.1
where the time goes:
time: 89.3 us; the launch traced here: 89.1 us
  waiting for transfers between devices  51.6 us (58%)
  matrix products  15.2 us (17%)
  between operations  13.5 us (15%)
  local copies, waits for them, and re-layouts  3.62 us (4%)
  starting transfers between devices  3.43 us (4%)
  other arithmetic  1.76 us (2%)
    all_gather x1, waiting for transfers between devices, attend(): shards = lax.all_gather(pair_shard[0], 'ctx', axis=0, tiled=True)  28 us
    ppermute x1, waiting for transfers between devices, from_behind(): lax.ppermute(value, axis, [(i, (i + by) % size) for i in range(size)])  13.8 us
    dot_general x1, matrix products, local(): jnp.dot(attended.reshape(rows_here, -1), out_proj[0].reshape(-1, out_proj...  11.7 us
    reduce_scatter x1, waiting for transfers between devices, local(): lax.psum_scatter(partial_sum.astype(jnp.bfloat16), 'tp', scatter_dimensio...  9.74 us
    ppermute x1, starting transfers between devices, from_behind(): lax.ppermute(value, axis, [(i, (i + by) % size) for i in range(size)])  3.38 us
    unnamed x6, local copies, waits for them, and re-layouts  3.29 us
    dot_general x1, matrix products, update(): jnp.einsum('rhgd,khd->hgrk', query_heads, key_block[:, :, :head_dim], pre...  2.02 us
  transfers between devices with their start and end apart: 3, of which 3 were waited for; matrix products, arithmetic and copies ran while one was open for 2% of the time, Pallas kernels for 0%

commit v1 on v0

--- a/solution.py
+++ b/solution.py
@@ -3,6 +3,33 @@
 import jax.numpy as jnp
 from jax import lax
 from jax.sharding import PartitionSpec as P
+
+
+def arrange_digits(along_axis, content):
+    wide_out = jax.lax.axis_size(along_axis)
+    x_now, w_next, finding = (wide_out, jax.lax.axis_index(along_axis), content.shape[0])
+    grid = [q * x_now if hop_no == 0 else q for hop_no, q in enumerate(content.shape)]
+    b_next = lax.dynamic_update_slice_in_dim(
+        jnp.zeros(grid, content.dtype), content, w_next * finding, axis=0
+    )
+    even = d_next = content
+    for tick in range(1, x_now // 2 + 1):
+        even = jax.lax.ppermute(
+            even,
+            axis_name=along_axis,
+            perm=list(map(lambda hop_no: (hop_no, (hop_no + 1) % x_now), range(x_now))),
+        )
+        b_next = lax.dynamic_update_slice_in_dim(
+            b_next, even, (w_next - tick) % x_now * finding, axis=0
+        )
+        if 2 * tick < x_now:
+            v_now = map(lambda hop_no: (hop_no, (hop_no - 1) % x_now), range(x_now))
+            outcome_arr = list(v_now)
+            d_next = jax.lax.ppermute(d_next, axis_name=along_axis, perm=outcome_arr)
+            b_next = lax.dynamic_update_slice_in_dim(
+                b_next, d_next, (w_next + tick) % x_now * finding, axis=0
+            )
+    return b_next
 
 
 def from_behind(value, axis, by):
@@ -62,7 +89,7 @@
         jnp.zeros((local_heads, group_size, rows_here), jnp.float32),
         jnp.zeros((local_heads, group_size, rows_here, head_dim), jnp.float32),
     )
-    shards = lax.all_gather(pair_shard[0], "ctx", axis=0, tiled=True)
+    shards = arrange_digits("ctx", pair_shard[0])
     shard_rows = shards.shape[0]
     block_len = math.gcd(shard_rows, 512)
 

time: 89.3 us -> 78.7 us (0.88)
  waiting for transfers between devices: 51.6 us -> 36.1 us
  starting transfers between devices: 3.43 us -> 8.95 us
  matrix products: 15.2 us -> 14.1 us
    all_gather x1 -> x0, waiting for transfers between devices: 28 us -> none  [attend(): shards = lax.all_gather(pair_shard[0], 'ctx', axis=0, tiled=True)]
    ppermute x0 -> x3, waiting for transfers between devices: none -> 13.1 us  [the longest x2 9.87 us: arrange_digits(): jax.lax.ppermute(even, axis_name=along_axis, perm=list(map(lambda hop_no:...]
    ppermute x0 -> x3, starting transfers between devices: none -> 5.1 us  [the longest x2 4.08 us: arrange_digits(): jax.lax.ppermute(even, axis_name=along_axis, perm=list(map(lambda hop_no:...]
    dot_general x1, matrix products: 2.02 us -> 0.92 us  [update(): jnp.einsum('rhgd,khd->hgrk', query_heads, key_block[:, :, :head_dim], pre...]
    dynamic_update_slice x0 -> x4, local copies, waits for them, and re-layouts: none -> 1.05 us  [the longest x1 0.99 us: arrange_digits(): lax.dynamic_update_slice_in_dim(jnp.zeros(grid, content.dtype), content,...]
    unnamed x6 -> x4, local copies, waits for them, and re-layouts: 3.29 us -> 2.6 us
  transfers between devices with their start and end apart: 3 -> 5, of which waited for: 3 -> 5; matrix products, arithmetic and copies ran while one was open for 2% -> 4% of each run, Pallas kernels for 0% -> 0%
where the time goes in v1:
time: 78.7 us; the launch traced here: 78.5 us
  waiting for transfers between devices  36.1 us (46%)
  matrix products  14.1 us (18%)
  between operations  13.5 us (17%)
  starting transfers between devices  8.95 us (11%)
  local copies, waits for them, and re-layouts  4.05 us (5%)
  other arithmetic  1.76 us (2%)
    ppermute x1, waiting for transfers between devices, from_behind(): lax.ppermute(value, axis, [(i, (i + by) % size) for i in range(size)])  13.1 us
    dot_general x1, matrix products, local(): jnp.dot(attended.reshape(rows_here, -1), out_proj[0].reshape(-1, out_proj...  11.7 us
    ppermute x2, waiting for transfers between devices, arrange_digits(): jax.lax.ppermute(even, axis_name=along_axis, perm=list(map(lambda hop_no:...  9.87 us
    reduce_scatter x1, waiting for transfers between devices, local(): lax.psum_scatter(partial_sum.astype(jnp.bfloat16), 'tp', scatter_dimensio...  9.82 us
    ppermute x2, starting transfers between devices, arrange_digits(): jax.lax.ppermute(even, axis_name=along_axis, perm=list(map(lambda hop_no:...  4.08 us
    ppermute x1, starting transfers between devices, from_behind(): lax.ppermute(value, axis, [(i, (i + by) % size) for i in range(size)])  3.85 us
    ppermute x1, waiting for transfers between devices, arrange_digits(): d_next = jax.lax.ppermute(d_next, axis_name=along_axis, perm=outcome_arr)  3.23 us
    unnamed x4, local copies, waits for them, and re-layouts  2.6 us
  transfers between devices with their start and end apart: 5, of which 5 were waited for; matrix products, arithmetic and copies ran while one was open for 4% of the time, Pallas kernels for 0%

profile of v1, /device:TPU:0, one launch (start us, length us, event | category | flops | bytes accessed | tf_op | source)
XLA Modules:
  0.0 78.5 jit_solution(12918237970220569508)
XLA Ops:
  6.5 0.0 copy-start
  6.5 0.0 reduce-scatter.2.cloned.1.call-start
  6.5 1.0 %copy.31 = bf16[1,128,4,256]{3,1,2,0:T(8,128)(2,1)S(1)} copy(bf16[1,128,4,256]{3,2,1,0:T(4,128)(2,1)} %param.5) | data formatting | bytes 524288 | tf_op args[1]
  7.5 3.0 %collective-permute-start = (bf16[128,4,256]{2,0,1:T(8,128)(2,1)S(1)}, bf16[128,4,256]{2,0,1:T(8,128)(2,1)S(1)}, u32[]{:S(2)}, u32[]{:S(2)}) collective-permute-start(bf16[128,4,256]{2,0,1:T(8,128)(2,1)S(1)} %bitcast.69), channel_id=1, source_target_pairs={{0,2},{2,4},{4,6},{6,0},{1,3},{3,5},{5,7},{7,1},{8,10},{10,12},{12... | collective-permute-start | bytes 786440 | tf_op jit(solution)/shard_map/ppermute | solution.py:17
  10.6 1.0 %collective-permute-start.1 = (bf16[128,4,256]{2,0,1:T(8,128)(2,1)S(1)}, bf16[128,4,256]{2,0,1:T(8,128)(2,1)S(1)}, u32[]{:S(2)}, u32[]{:S(2)}) collective-permute-start(bf16[128,4,256]{2,0,1:T(8,128)(2,1)S(1)} %bitcast.70), channel_id=1, source_target_pairs={{0,6},{2,0},{4,2},{6,4},{1,7},{3,1},{5,3},{7,5},{8,14},{10,8},{12,... | collective-permute-start | bytes 786440 | tf_op jit(solution)/shard_map/ppermute | solution.py:28
  11.6 0.0 copy-done
  11.6 0.2 reduce-window.8
  11.8 0.1 convert_reduce_fusion.1
  11.9 0.1 convert_reduce_fusion
  11.9 0.1 broadcast_in_dim.47
  12.0 1.0 %constant_dynamic-update-slice_fusion.3 = bf16[512,4,256]{2,0,1:T(8,128)(2,1)S(1)} fusion(bf16[512,4,256]{2,0,1:T(8,128)(2,1)S(1)} %broadcast_in_dim.47, s32[]{:T(128)S(6)} %select_n.42, bf16[1,128,4,256]{3,2,1,0:T(4,128)(2,1)} %param.5), kind=kLoop, calls=%fused_computation.30 | loop fusion | bytes 524292 | tf_op jit(solution)/shard_map/dynamic_update_slice | solution.py:12
  13.0 5.7 %collective-permute-done = bf16[128,4,256]{2,0,1:T(8,128)(2,1)S(1)} collective-permute-done((bf16[128,4,256]{2,0,1:T(8,128)(2,1)S(1)}, bf16[128,4,256]{2,0,1:T(8,128)(2,1)S(1)}, u32[]{:S(2)}, u32[]{:S(2)}) %collective-permute-start) | collective-permute-done | bytes 262176 | tf_op jit(solution)/shard_map/ppermute | solution.py:17
  18.7 1.1 %collective-permute-start.2 = (bf16[128,4,256]{2,0,1:T(8,128)(2,1)S(1)}, bf16[128,4,256]{2,0,1:T(8,128)(2,1)S(1)}, u32[]{:S(2)}, u32[]{:S(2)}) collective-permute-start(bf16[128,4,256]{2,0,1:T(8,128)(2,1)S(1)} %collective-permute-done), channel_id=1, source_target_pairs={{0,2},{2,4},{4,6},{6,0},{1,3},{3,5},{5,7},{7,1},{8,10},{10,12},{12... | collective-permute-start | bytes 786440 | tf_op jit(solution)/shard_map/ppermute | solution.py:17
  19.7 0.1 fusion.24
  19.9 1.6 %copy.17 = bf16[1,128,4,640]{1,3,2,0:T(8,128)(2,1)S(1)} copy(bf16[1,128,4,640]{3,2,1,0:T(4,128)(2,1)} %param.4) | data formatting | bytes 1310720 | tf_op args[0]
  21.6 3.2 %collective-permute-done.1 = bf16[128,4,256]{2,0,1:T(8,128)(2,1)S(1)} collective-permute-done((bf16[128,4,256]{2,0,1:T(8,128)(2,1)S(1)}, bf16[128,4,256]{2,0,1:T(8,128)(2,1)S(1)}, u32[]{:S(2)}, u32[]{:S(2)}) %collective-permute-start.1) | collective-permute-done | bytes 262176 | tf_op jit(solution)/shard_map/ppermute | solution.py:28
  24.8 4.2 %collective-permute-done.2 = bf16[128,4,256]{2,0,1:T(8,128)(2,1)S(1)} collective-permute-done((bf16[128,4,256]{2,0,1:T(8,128)(2,1)S(1)}, bf16[128,4,256]{2,0,1:T(8,128)(2,1)S(1)}, u32[]{:S(2)}, u32[]{:S(2)}) %collective-permute-start.2) | collective-permute-done | bytes 262176 | tf_op jit(solution)/shard_map/ppermute | solution.py:17
  29.1 0.9 %fusion.8 = (f32[4,5,128]{2,1,0:T(8,128)S(1)}, f32[4,512,128,5]{2,1,3,0:T(8,128)S(1)}) fusion(pred[128,512]{0,1:T(8,128)(4,1)S(1)} %fusion.24, bf16[128,4,5,128]{0,3,2,1:T(8,128)(2,1)S(1)} %bitcast.67, bf16[512,4,256]{2,0,1:T(8,128)(2,1)S(1)} %constant_dynamic-update-slice_fusion), kind=kOutput, calls=%fused_computation.6 | convolution fusion | flops 339473920 | bytes 6498304 | tf_op jit(solution)/shard_map/while/body/eval_jaxpr/rhgd,khd->hgrk/dot_general | solution.py:65
  30.0 1.3 %fusion.9 = f32[4,5,128]{2,1,0:T(8,128)S(1)} fusion(f32[4,512,128,5]{2,1,3,0:T(8,128)S(1)} %get-tuple-element.26, f32[4,5,128]{2,1,0:T(8,128)S(1)} %get-tuple-element.24, pred[128,512]{0,1:T(8,128)(4,1)S(1)} %fusion.24), kind=kLoop, calls=%fused_computation.7 | loop fusion | flops 6551040 | bytes 5328896 | tf_op jit(solution)/shard_map/while/body/eval_jaxpr/reduce_sum | solution.py:77
  31.3 1.5 %divide_convert_fusion = bf16[128,4,5,128]{0,3,2,1:T(8,128)(2,1)S(1)} fusion(f32[4,512,128,5]{2,1,3,0:T(8,128)S(1)} %get-tuple-element.26, f32[4,5,128]{2,1,0:T(8,128)S(1)} %get-tuple-element.24, pred[128,512]{0,1:T(8,128)(4,1)S(1)} %fusion.24, f32[128,4,5]{0,2,1:T(8,128)S(1)} %bitcast_add_fusion, f32[128,4,5]{0,2,1:T(8,128)S(1)} %get-tuple-element.23, ...), kind=kOutput, calls=%fused_computation.13 | convolution fusion | flops 343080960 | bytes 6537216 | tf_op jit(solution)/shard_map/while/body/eval_jaxpr/hgrk,khd->hgrd/dot_general | solution.py:78
  32.8 0.3 copy.21
  33.1 3.8 %collective-permute-start.3 = (bf16[1,128,4,640]{3,1,2,0:T(8,128)(2,1)S(1)}, bf16[1,128,4,640]{3,1,2,0:T(8,128)(2,1)S(1)}, u32[]{:S(2)}, u32[]{:S(2)}) collective-permute-start(bf16[1,128,4,640]{3,1,2,0:T(8,128)(2,1)S(1)} %copy.21), channel_id=1, source_target_pairs={{0,24},{8,0},{16,8},{24,16},{1,25},{9,1},{17,9},{25,17},{2,26},{10... | collective-permute-start | bytes 1966088 | tf_op jit(solution)/shard_map/ppermute | solution.py:37
  37.0 13.1 %collective-permute-done.3 = bf16[1,128,4,640]{3,1,2,0:T(8,128)(2,1)S(1)} collective-permute-done((bf16[1,128,4,640]{3,1,2,0:T(8,128)(2,1)S(1)}, bf16[1,128,4,640]{3,1,2,0:T(8,128)(2,1)S(1)}, u32[]{:S(2)}, u32[]{:S(2)}) %collective-permute-start.3) | collective-permute-done | bytes 655392 | tf_op jit(solution)/shard_map/ppermute | solution.py:37
  50.1 11.7 %fusion.5 = bf16[128,5120]{1,0:T(8,128)(2,1)} fusion(bf16[1,4,640,5120]{3,2,1,0:T(8,128)(2,1)} %param.6, bf16[1,128,4,640]{3,1,2,0:T(8,128)(2,1)S(1)} %collective-permute-done.3), kind=kOutput, calls=%fused_computation.3 | convolution fusion | flops 3356098560 | bytes 28180480 | tf_op jit(solution)/shard_map/dot_general | solution.py:113
  61.8 0.0 reduce-scatter.2.cloned.1.call-update
  61.9 9.8 %reduce-scatter.2.cloned.1.call-done = bf16[128,2560]{1,0:T(8,128)(2,1)} async-done(((bf16[128,5120]{1,0:T(8,128)(2,1)}), bf16[128,2560]{1,0:T(8,128)(2,1)}) %reduce-scatter.2.cloned.1.call-update) | async-done | bytes 655376 | tf_op jit(solution)/shard_map/reduce_scatter | solution.py:118
  (7 shorter events, 0.1 us)
Async XLA Ops:
  6.5 5.0 %copy-start = (s32[4,4]{1,0:T(4,128)S(1)}, s32[4,4]{1,0:T(4,128)}, u32[]{:S(2)}) copy-start(s32[4,4]{1,0:T(4,128)} %param.7) | copy-start | bytes 196
  6.5 65.1 %reduce-scatter.2.cloned.1.call-start = ((), (), s32[]{:S(2)}) async-start(), calls=%async_computation.1 | async-start | bytes 1966080 | tf_op jit(solution)/shard_map/reduce_scatter | solution.py:118
  7.5 11.1 %collective-permute-start = (bf16[128,4,256]{2,0,1:T(8,128)(2,1)S(1)}, bf16[128,4,256]{2,0,1:T(8,128)(2,1)S(1)}, u32[]{:S(2)}, u32[]{:S(2)}) collective-permute-start(bf16[128,4,256]{2,0,1:T(8,128)(2,1)S(1)} %bitcast.69), channel_id=1, source_target_pairs={{0,2},{2,4},{4,6},{6,0},{1,3},{3,5},{5,7},{7,1},{8,10},{10,12},{12... | collective-permute-start | bytes 786440 | tf_op jit(solution)/shard_map/ppermute | solution.py:17
  10.6 14.3 %collective-permute-start.1 = (bf16[128,4,256]{2,0,1:T(8,128)(2,1)S(1)}, bf16[128,4,256]{2,0,1:T(8,128)(2,1)S(1)}, u32[]{:S(2)}, u32[]{:S(2)}) collective-permute-start(bf16[128,4,256]{2,0,1:T(8,128)(2,1)S(1)} %bitcast.70), channel_id=1, source_target_pairs={{0,6},{2,0},{4,2},{6,4},{1,7},{3,1},{5,3},{7,5},{8,14},{10,8},{12,... | collective-permute-start | bytes 786440 | tf_op jit(solution)/shard_map/ppermute | solution.py:28
  18.7 10.4 %collective-permute-start.2 = (bf16[128,4,256]{2,0,1:T(8,128)(2,1)S(1)}, bf16[128,4,256]{2,0,1:T(8,128)(2,1)S(1)}, u32[]{:S(2)}, u32[]{:S(2)}) collective-permute-start(bf16[128,4,256]{2,0,1:T(8,128)(2,1)S(1)} %collective-permute-done), channel_id=1, source_target_pairs={{0,2},{2,4},{4,6},{6,0},{1,3},{3,5},{5,7},{7,1},{8,10},{10,12},{12... | collective-permute-start | bytes 786440 | tf_op jit(solution)/shard_map/ppermute | solution.py:17
  33.1 17.0 %collective-permute-start.3 = (bf16[1,128,4,640]{3,1,2,0:T(8,128)(2,1)S(1)}, bf16[1,128,4,640]{3,1,2,0:T(8,128)(2,1)S(1)}, u32[]{:S(2)}, u32[]{:S(2)}) collective-permute-start(bf16[1,128,4,640]{3,1,2,0:T(8,128)(2,1)S(1)} %copy.21), channel_id=1, source_target_pairs={{0,24},{8,0},{16,8},{24,16},{1,25},{9,1},{17,9},{25,17},{2,26},{10... | collective-permute-start | bytes 1966088 | tf_op jit(solution)/shard_map/ppermute | solution.py:37
Sparse Core Ops, SparseCore 0:
  62.0 9.6 reduce-scatter.1
